TPU v7x, 32 devices: a whole 2x2x4 slice. The times are simulated.
32 devices in a mesh: blk: 8 (over y, x, core), head: 4 (over z).
Axes of the slice: x: 2, y: 2, z: 4, core: 2. Of those that a mesh axis runs over, the one named last changes fastest.
Arguments:
- hidden_in: float32 [2, 2048, 2048], P(None, ('blk', 'head')), may hold values from -6 to 6
- span_order: int32 [16], replicated, may hold values from 0 to 15, each once
- attn_gain: bfloat16 [1, 2048], P(None, ('blk', 'head')), may hold values from 0.099609375 to 1.8984375
- w_query: bfloat16 [1, 2048, 2048], P(None, ('blk', 'head')), may hold values from -0.125 to 0.125
- w_key: bfloat16 [1, 2048, 256], P(None, ('blk', 'head')), may hold values from -0.125 to 0.125
- w_value: bfloat16 [1, 2048, 256], P(None, ('blk', 'head')), may hold values from -0.125 to 0.125
- w_out: bfloat16 [1, 2048, 2048], P(None, ('blk', 'head')), may hold values from -1.5 to 1.5
- ffn_gain: bfloat16 [1, 2048], P(None, ('blk', 'head')), may hold values from 0.099609375 to 1.8984375
- w_gate: bfloat16 [1, 2048, 5632], P(None, 'blk', 'head'), may hold values from -0.125 to 0.125
- w_up: bfloat16 [1, 2048, 5632], P(None, 'blk', 'head'), may hold values from -0.125 to 0.125
- w_down: bfloat16 [1, 5632, 2048], P(None, 'head', 'blk'), may hold values from -0.078125 to 0.078125
- cotangent: float32 [2, 2048, 2048], P(None, ('blk', 'head')), may hold values from -6 to 6
Outputs:
- hidden_out: float32 [2, 2048, 2048], P(None, ('blk', 'head'))
- grad_in: float32 [2, 2048, 2048], P(None, ('blk', 'head'))
- grad_attn_gain: float32 [1, 2048], P(None, ('blk', 'head'))
- grad_query_w: float32 [1, 2048, 2048], P(None, ('blk', 'head'))
- grad_key_w: float32 [1, 2048, 256], P(None, ('blk', 'head'))
- grad_value_w: float32 [1, 2048, 256], P(None, ('blk', 'head'))
- grad_out_w: float32 [1, 2048, 2048], P(None, ('blk', 'head'))
- grad_ffn_gain: float32 [1, 2048], P(None, ('blk', 'head'))
- gate_weight_gradient: float32 [1, 2048, 5632], P(None, 'blk', 'head')
- grad_up_w: float32 [1, 2048, 5632], P(None, 'blk', 'head')
- grad_down_w: float32 [1, 5632, 2048], P(None, 'head', 'blk')
Inputs may be any that keep to these rules, and one draw needn't show every extreme that they name: A permutation: stored span j of each sequence (stored tokens j * 128 to (j + 1) * 128 - 1) is span span_order[j] of the sequence.
All inputs are finite; a program needn't handle non-finite values.
Results may differ from a plain program's by a relative error of at most 0.02.
Values may be sent and summed in bfloat16 or wider, within the bound.
No kernel may reach another device: no remote copies, remote signals or barrier semaphores. Data moves between devices by JAX's collectives and lax.ppermute only.
A program may use at most 192 MiB of HBM per device.

v0:
```python
import jax
import jax.numpy as jnp
from jax import lax
from jax.sharding import PartitionSpec as P

HEADS = 32
KV_HEADS = 4
HEAD_DIM = 64


EPS = 1e-05
THETA = 10000.0
NEGATIVE_PADDING = -1e30


def from_behind(shard, axis, by):
    devices = lax.axis_size(axis)
    return lax.ppermute(shard, axis, [(i, (i + by) % devices) for i in range(devices)])


def rope_angles(positions, half_dim):
    inverse = 1.0 / THETA ** (jnp.arange(half_dim, dtype=jnp.float32) * (2.0 / (2 * half_dim)))
    angles = positions.astype(jnp.float32)[:, None] * inverse[None, :]
    return (jnp.cos(angles), jnp.sin(angles))


def rotate_forward(values, cosine_table, sine_table):
    half_dim = values.shape[-1] // 2
    first_half = values[..., :half_dim]
    second_half = values[..., half_dim:]
    cos_part = cosine_table[:, None, :]
    sin_part = sine_table[:, None, :]
    return jnp.concatenate(
        [
            first_half * cos_part - second_half * sin_part,
            second_half * cos_part + first_half * sin_part,
        ],
        axis=-1,
    )


def rotate_backward(gradients, cosine_table, sine_table):
    half_dim = gradients.shape[-1] // 2
    first_half = gradients[..., :half_dim]
    second_half = gradients[..., half_dim:]
    cos_part = cosine_table[:, None, :]
    sin_part = sine_table[:, None, :]
    return jnp.concatenate(
        [
            first_half * cos_part + second_half * sin_part,
            second_half * cos_part - first_half * sin_part,
        ],
        axis=-1,
    )


def rms_forward(values, gain_values):
    inverse_rms = lax.rsqrt(jnp.mean(values * values, axis=-1, keepdims=True) + EPS)
    unit_values = values * inverse_rms
    return (unit_values * gain_values, unit_values, inverse_rms)


def rms_backward(grad_normed, unit_values, inverse_rms, gain_values):
    grad_unit = grad_normed * gain_values
    value_gradient_list = inverse_rms * (
        grad_unit - unit_values * jnp.mean(grad_unit * unit_values, axis=-1, keepdims=True)
    )
    grad_gain = jnp.sum(grad_normed * unit_values, axis=(0, 1))
    return (value_gradient_list, grad_gain)


def lookup_order(span_order, span_ids):
    matches = span_ids[:, None] == jnp.arange(span_order.shape[0], dtype=jnp.int32)[None, :]
    return jnp.sum(jnp.where(matches, span_order[None, :], 0), axis=1)


def true_positions(span_order, start_index, token_count, span_len):
    token_index = start_index + jnp.arange(token_count, dtype=jnp.int32)
    return lookup_order(span_order, token_index // span_len) * span_len + token_index % span_len


def gather_attention(gain_one, query_w, key_w, value_w, out_w, gain_two):
    return (
        lax.all_gather(gain_one, ("blk", "head"), axis=0, tiled=True),
        lax.all_gather(query_w, ("blk", "head"), axis=0, tiled=True),
        lax.all_gather(key_w, ("blk", "head"), axis=0, tiled=True),
        lax.all_gather(value_w, ("blk", "head"), axis=0, tiled=True),
        lax.all_gather(out_w, ("blk", "head"), axis=0, tiled=True),
        lax.all_gather(gain_two, ("blk", "head"), axis=0, tiled=True),
    )


def gather_ffn(gate_w, up_w, down_w):
    return (
        lax.all_gather(gate_w, "blk", axis=0, tiled=True),
        lax.all_gather(up_w, "blk", axis=0, tiled=True),
        lax.all_gather(down_w, "blk", axis=1, tiled=True),
    )


def cycle_forward(query_heads, kv_heads, span_order, score_scale):
    seq_count, block_rows, query_width = query_heads.shape
    head_dim = kv_heads.shape[2] // 2
    per_device = query_width // head_dim
    span_len = block_rows // 2
    cycle_size = lax.axis_size("blk")
    cycle_pos = lax.axis_index("blk")
    queries = query_heads.reshape(seq_count, 2, span_len, per_device, head_dim)
    own_orders = lookup_order(span_order, 2 * cycle_pos + jnp.arange(2, dtype=jnp.int32))
    offsets = jnp.arange(span_len, dtype=jnp.int32)

    def absorb(states, kv_block, source):
        key_orders = lookup_order(span_order, 2 * source + jnp.arange(2, dtype=jnp.int32))
        updated = []
        for query_part in range(2):
            state_now = states[query_part]
            for key_part in range(2):

                def attend(carried, query_part=query_part, key_part=key_part):
                    row_top, row_total, accumulated = carried
                    key_block = kv_block[
                        :, key_part * span_len : (key_part + 1) * span_len, :head_dim
                    ]
                    value_tile_rows = kv_block[
                        :, key_part * span_len : (key_part + 1) * span_len, head_dim:
                    ]
                    scores = (
                        jnp.einsum(
                            "tzgf,tof->tgzo",
                            queries[:, query_part],
                            key_block,
                            preferred_element_type=jnp.float32,
                        )
                        * score_scale
                    )
                    query_pos = own_orders[query_part] * span_len + offsets
                    key_pos = key_orders[key_part] * span_len + offsets
                    allowed = key_pos[None, :] <= query_pos[:, None]
                    scores = jnp.where(allowed[None, None], scores, NEGATIVE_PADDING)
                    new_top = jnp.maximum(row_top, jnp.max(scores, axis=-1))
                    weights = jnp.exp(scores - new_top[..., None])
                    factor = jnp.exp(row_top - new_top)
                    row_total = row_total * factor + jnp.sum(weights, axis=-1)
                    contribution = jnp.einsum(
                        "nyfm,nma->nfya",
                        weights.astype(jnp.bfloat16),
                        value_tile_rows,
                        preferred_element_type=jnp.float32,
                    )
                    accumulated = (
                        accumulated * jnp.transpose(factor, (0, 2, 1))[..., None] + contribution
                    )
                    return (new_top, row_total, accumulated)

                state_now = lax.cond(
                    key_orders[key_part] <= own_orders[query_part],
                    attend,
                    lambda carried: carried,
                    state_now,
                )
            updated.append(state_now)
        return tuple(updated)

    initial = (
        jnp.full((seq_count, per_device, span_len), NEGATIVE_PADDING, jnp.float32),
        jnp.zeros((seq_count, per_device, span_len), jnp.float32),
        jnp.zeros((seq_count, span_len, per_device, head_dim), jnp.float32),
    )
    states = absorb((initial, initial), kv_heads, cycle_pos)
    stored = jnp.zeros((cycle_size,) + kv_heads.shape, kv_heads.dtype)
    stored = lax.dynamic_update_index_in_dim(stored, kv_heads, 0, 0)

    def cycle_step(step_index, carried):
        kv_block, states_now, stored_now = carried
        kv_block = from_behind(kv_block, "blk", 1)
        source = (cycle_pos - step_index) % cycle_size
        states_now = absorb(states_now, kv_block, source)
        stored_now = lax.dynamic_update_index_in_dim(stored_now, kv_block, step_index, 0)
        return (kv_block, states_now, stored_now)

    kv_last, states, stored = lax.fori_loop(1, cycle_size, cycle_step, (kv_heads, states, stored))
    outputs = []
    log_totals = []
    for query_part in range(2):
        row_top, row_total, accumulated = states[query_part]
        outputs.append(accumulated / jnp.transpose(row_total, (0, 2, 1))[..., None])
        log_totals.append(row_top + jnp.log(row_total))
    attended = (
        jnp.stack(outputs, axis=1).reshape(seq_count, block_rows, query_width).astype(jnp.bfloat16)
    )
    return (attended, jnp.stack(log_totals, axis=0), stored)


def cycle_backward(query_heads, out_heads, grad_heads, log_totals, stored, span_order, score_scale):
    seq_count, block_rows, query_width = query_heads.shape
    head_dim = stored.shape[-1] // 2
    per_device = query_width // head_dim
    span_len = block_rows // 2
    cycle_size = lax.axis_size("blk")
    cycle_pos = lax.axis_index("blk")
    queries = query_heads.reshape(seq_count, 2, span_len, per_device, head_dim)
    grad_rows_all = grad_heads.reshape(seq_count, 2, span_len, per_device, head_dim)
    out_rows = out_heads.reshape(seq_count, 2, span_len, per_device, head_dim)
    row_delta = jnp.transpose(
        jnp.sum(grad_rows_all.astype(jnp.float32) * out_rows.astype(jnp.float32), axis=-1),
        (0, 1, 3, 2),
    )
    own_orders = lookup_order(span_order, 2 * cycle_pos + jnp.arange(2, dtype=jnp.int32))
    offsets = jnp.arange(span_len, dtype=jnp.int32)

    def emit(carried_pair, kv_block, source):
        key_orders = lookup_order(span_order, 2 * source + jnp.arange(2, dtype=jnp.int32))
        for query_part in range(2):
            for key_part in range(2):

                def backprop(carried, query_part=query_part, key_part=key_part):
                    grad_query, grad_kv = carried
                    key_block = kv_block[
                        :, key_part * span_len : (key_part + 1) * span_len, :head_dim
                    ]
                    value_tile_rows = kv_block[
                        :, key_part * span_len : (key_part + 1) * span_len, head_dim:
                    ]
                    scores = (
                        jnp.einsum(
                            "tzgf,tof->tgzo",
                            queries[:, query_part],
                            key_block,
                            preferred_element_type=jnp.float32,
                        )
                        * score_scale
                    )
                    query_pos = own_orders[query_part] * span_len + offsets
                    key_pos = key_orders[key_part] * span_len + offsets
                    allowed = key_pos[None, :] <= query_pos[:, None]
                    scores = jnp.where(allowed[None, None], scores, NEGATIVE_PADDING)
                    probabilities = jnp.exp(scores - log_totals[query_part][..., None])
                    gradient_row_block = grad_rows_all[:, query_part]
                    value_grad = jnp.einsum(
                        "iwfm,ifwy->imy",
                        probabilities.astype(jnp.bfloat16),
                        gradient_row_block,
                        preferred_element_type=jnp.float32,
                    )
                    prob_grad = jnp.einsum(
                        "tzgf,tof->tgzo",
                        gradient_row_block,
                        value_tile_rows,
                        preferred_element_type=jnp.float32,
                    )
                    score_grad = (
                        probabilities * (prob_grad - row_delta[:, query_part][..., None])
                    ).astype(jnp.bfloat16)
                    query_add = (
                        jnp.einsum(
                            "nyfm,nma->nfya",
                            score_grad,
                            key_block,
                            preferred_element_type=jnp.float32,
                        )
                        * score_scale
                    )
                    key_add = (
                        jnp.einsum(
                            "iwfm,ifwy->imy",
                            score_grad,
                            queries[:, query_part],
                            preferred_element_type=jnp.float32,
                        )
                        * score_scale
                    )
                    grad_query = grad_query.at[:, query_part].add(query_add)
                    grad_kv = grad_kv.at[:, key_part * span_len : (key_part + 1) * span_len].add(
                        jnp.concatenate([key_add, value_grad], axis=-1)
                    )
                    return (grad_query, grad_kv)

                carried_pair = lax.cond(
                    key_orders[key_part] <= own_orders[query_part],
                    backprop,
                    lambda carried: carried,
                    carried_pair,
                )
        return carried_pair

    def cycle_step(step_index, carried):
        grad_query, grad_kv = carried
        kv_block = lax.dynamic_index_in_dim(stored, step_index, 0, keepdims=False)
        source = (cycle_pos - step_index) % cycle_size
        grad_query, grad_kv = emit((grad_query, grad_kv), kv_block, source)
        grad_kv = from_behind(grad_kv.astype(jnp.bfloat16), "blk", 1).astype(grad_kv.dtype)
        return (grad_query, grad_kv)

    start_query = jnp.zeros((seq_count, 2, span_len, per_device, head_dim), jnp.float32)
    start_kv = jnp.zeros((seq_count, block_rows, 2 * head_dim), jnp.float32)
    return lax.fori_loop(0, cycle_size, cycle_step, (start_query, start_kv))


def on_device(
    hidden_in,
    span_order,
    attn_gain,
    w_query,
    w_key,
    w_value,
    w_out,
    ffn_gain,
    w_gate,
    w_up,
    w_down,
    cotangent,
):
    seq_count, tok_dev, model_width = hidden_in.shape
    layer_count = w_query.shape[0]
    group_size = lax.axis_size("head")
    group_pos = lax.axis_index("head")
    cycle_pos = lax.axis_index("blk")
    span_len = tok_dev * group_size // 2
    per_device = HEADS // group_size
    repeat_count = group_size // KV_HEADS
    score_scale = HEAD_DIM ** (-0.5)
    local_pos = true_positions(
        span_order, (cycle_pos * group_size + group_pos) * tok_dev, tok_dev, span_len
    )
    block_pos = true_positions(span_order, cycle_pos * 2 * span_len, 2 * span_len, span_len)
    local_cos, local_sin = rope_angles(local_pos, HEAD_DIM // 2)
    block_cos, block_sin = rope_angles(block_pos, HEAD_DIM // 2)
    token_rows = seq_count * tok_dev
    kept_weights = []
    current = hidden_in
    layer_index = 0
    attn_full = gather_attention(
        attn_gain[layer_index],
        w_query[layer_index],
        w_key[layer_index],
        w_value[layer_index],
        w_out[layer_index],
        ffn_gain[layer_index],
    )
    gain_one, query_w, key_w, value_w, out_w, gain_two = attn_full
    normed_one, unit_one, inverse_one = rms_forward(current, gain_one.astype(jnp.float32))
    flat_one = normed_one.astype(jnp.bfloat16).reshape(token_rows, model_width)
    query = jnp.dot(flat_one, query_w, preferred_element_type=jnp.float32).reshape(
        seq_count, tok_dev, HEADS, HEAD_DIM
    )
    key_proj = jnp.dot(flat_one, key_w, preferred_element_type=jnp.float32).reshape(
        seq_count, tok_dev, KV_HEADS, HEAD_DIM
    )
    value_proj = jnp.dot(flat_one, value_w, preferred_element_type=jnp.float32).reshape(
        seq_count, tok_dev, KV_HEADS, HEAD_DIM
    )
    query = rotate_forward(query, local_cos, local_sin).astype(jnp.bfloat16)
    key_proj = rotate_forward(key_proj, local_cos, local_sin).astype(jnp.bfloat16)
    paired = jnp.concatenate([key_proj, value_proj.astype(jnp.bfloat16)], axis=-1)
    paired = jnp.repeat(paired, repeat_count, axis=2)
    query_heads = lax.all_to_all(
        query.reshape(seq_count, tok_dev, group_size, per_device * HEAD_DIM),
        "head",
        split_axis=2,
        concat_axis=1,
        tiled=True,
    )
    kv_heads = lax.all_to_all(paired, "head", split_axis=2, concat_axis=1, tiled=True)
    query_heads = query_heads.reshape(seq_count, 2 * span_len, per_device * HEAD_DIM)
    kv_heads = kv_heads.reshape(seq_count, 2 * span_len, 2 * HEAD_DIM)
    out_heads, log_totals, stored = cycle_forward(query_heads, kv_heads, span_order, score_scale)
    attended = lax.all_to_all(
        out_heads.reshape(seq_count, 2 * span_len, 1, per_device * HEAD_DIM),
        "head",
        split_axis=1,
        concat_axis=2,
        tiled=True,
    )
    attended = attended.reshape(token_rows, HEADS * HEAD_DIM)
    middle_hidden = current + jnp.dot(attended, out_w, preferred_element_type=jnp.float32).reshape(
        seq_count, tok_dev, model_width
    )
    normed_two, unit_two, inverse_two = rms_forward(middle_hidden, gain_two.astype(jnp.float32))
    group_rows = lax.all_gather(
        normed_two.astype(jnp.bfloat16), "head", axis=1, tiled=True
    ).reshape(-1, model_width)
    ffn_full = gather_ffn(w_gate[layer_index], w_up[layer_index], w_down[layer_index])
    gate_w, up_w, down_w = ffn_full
    gate_act = jnp.dot(group_rows, gate_w, preferred_element_type=jnp.float32)
    up_act = jnp.dot(group_rows, up_w, preferred_element_type=jnp.float32)
    activated = (jax.nn.silu(gate_act) * up_act).astype(jnp.bfloat16)
    partial_out = jnp.dot(activated, down_w, preferred_element_type=jnp.float32).reshape(
        seq_count, group_size * tok_dev, model_width
    )
    current = middle_hidden + lax.psum_scatter(
        partial_out.astype(jnp.bfloat16), "head", scatter_dimension=1, tiled=True
    ).astype(jnp.float32)
    saved = [
        (
            flat_one,
            unit_one,
            inverse_one,
            query_heads,
            out_heads,
            log_totals,
            stored,
            attended,
            unit_two,
            inverse_two,
            group_rows,
            gate_act,
            up_act,
            activated,
        )
    ]
    kept_weights.append((attn_full, ffn_full))
    upstream = cotangent
    attn_results = [None] * layer_count
    ffn_results = [None] * layer_count
    for layer_index in reversed(range(layer_count)):
        (
            flat_one,
            unit_one,
            inverse_one,
            query_heads,
            out_heads,
            log_totals,
            stored,
            attended,
            unit_two,
            inverse_two,
            group_rows,
            gate_act,
            up_act,
            activated,
        ) = saved[layer_index]
        attn_full = gather_attention(
            attn_gain[layer_index],
            w_query[layer_index],
            w_key[layer_index],
            w_value[layer_index],
            w_out[layer_index],
            ffn_gain[layer_index],
        )
        ffn_full = gather_ffn(w_gate[layer_index], w_up[layer_index], w_down[layer_index])
        gain_one, query_w, key_w, value_w, out_w, gain_two = attn_full
        gate_w, up_w, down_w = ffn_full
        group_grad = lax.all_gather(
            upstream.astype(jnp.bfloat16), "head", axis=1, tiled=True
        ).reshape(-1, model_width)
        grad_activated = jnp.einsum(
            "rd,fd->rf", group_grad, down_w, preferred_element_type=jnp.float32
        )
        sigmoid_gate = jax.nn.sigmoid(gate_act)
        grad_gate = (
            grad_activated * up_act * sigmoid_gate * (1.0 + gate_act * (1.0 - sigmoid_gate))
        ).astype(jnp.bfloat16)
        grad_upper = (grad_activated * gate_act * sigmoid_gate).astype(jnp.bfloat16)
        term_down = jnp.einsum(
            "rf,rd->fd", activated, group_grad, preferred_element_type=jnp.float32
        )
        term_gate = jnp.einsum(
            "rd,rf->df", group_rows, grad_gate, preferred_element_type=jnp.float32
        )
        up_projection_term = jnp.einsum(
            "rd,rf->df", group_rows, grad_upper, preferred_element_type=jnp.float32
        )
        normed_part = jnp.einsum(
            "rf,df->rd", grad_gate, gate_w, preferred_element_type=jnp.float32
        ) + jnp.einsum("rf,df->rd", grad_upper, up_w, preferred_element_type=jnp.float32)
        grad_normed_two = lax.psum_scatter(
            normed_part.reshape(seq_count, group_size * tok_dev, model_width).astype(jnp.bfloat16),
            "head",
            scatter_dimension=1,
            tiled=True,
        ).astype(jnp.float32)
        ffn_results[layer_index] = (
            lax.psum_scatter(
                term_gate.astype(jnp.bfloat16), "blk", scatter_dimension=0, tiled=True
            ).astype(jnp.float32),
            lax.psum_scatter(
                up_projection_term.astype(jnp.bfloat16), "blk", scatter_dimension=0, tiled=True
            ).astype(jnp.float32),
            lax.psum_scatter(
                term_down.astype(jnp.bfloat16), "blk", scatter_dimension=1, tiled=True
            ).astype(jnp.float32),
        )
        grad_mid_part, gain_two_grad = rms_backward(
            grad_normed_two, unit_two, inverse_two, gain_two.astype(jnp.float32)
        )
        grad_middle = upstream + grad_mid_part
        grad_mid_low = grad_middle.astype(jnp.bfloat16).reshape(token_rows, model_width)
        term_out = jnp.einsum(
            "rq,rd->qd", attended, grad_mid_low, preferred_element_type=jnp.float32
        )
        grad_attended = jnp.einsum(
            "rd,qd->rq", grad_mid_low, out_w, preferred_element_type=jnp.float32
        ).astype(jnp.bfloat16)
        grad_heads = lax.all_to_all(
            grad_attended.reshape(seq_count, tok_dev, group_size, per_device * HEAD_DIM),
            "head",
            split_axis=2,
            concat_axis=1,
            tiled=True,
        )
        grad_heads = grad_heads.reshape(seq_count, 2 * span_len, per_device * HEAD_DIM)
        grad_query, grad_kv = cycle_backward(
            query_heads, out_heads, grad_heads, log_totals, stored, span_order, score_scale
        )
        grad_query = rotate_backward(
            grad_query.reshape(seq_count, 2 * span_len, per_device, HEAD_DIM), block_cos, block_sin
        )
        grad_key_rot = rotate_backward(grad_kv[:, :, None, :HEAD_DIM], block_cos, block_sin)[
            :, :, 0, :
        ]
        grad_kv = jnp.concatenate([grad_key_rot, grad_kv[..., HEAD_DIM:]], axis=-1)
        query_back, kv_back = (
            lax.all_to_all(
                grad_query.reshape(seq_count, 2 * span_len, 1, per_device * HEAD_DIM).astype(
                    jnp.bfloat16
                ),
                "head",
                split_axis=1,
                concat_axis=2,
                tiled=True,
            ).astype(jnp.float32),
            lax.all_to_all(
                grad_kv.reshape(seq_count, 2 * span_len, 1, 2 * HEAD_DIM).astype(jnp.bfloat16),
                "head",
                split_axis=1,
                concat_axis=2,
                tiled=True,
            ).astype(jnp.float32),
        )
        query_low = query_back.reshape(token_rows, HEADS * HEAD_DIM).astype(jnp.bfloat16)
        kv_summed = jnp.sum(
            kv_back.reshape(seq_count, tok_dev, KV_HEADS, repeat_count, 2 * HEAD_DIM), axis=3
        )
        key_low = (
            kv_summed[..., :HEAD_DIM].reshape(token_rows, KV_HEADS * HEAD_DIM).astype(jnp.bfloat16)
        )
        value_low = (
            kv_summed[..., HEAD_DIM:].reshape(token_rows, KV_HEADS * HEAD_DIM).astype(jnp.bfloat16)
        )
        term_query = jnp.einsum(
            "rd,rq->dq", flat_one, query_low, preferred_element_type=jnp.float32
        )
        term_key = jnp.einsum("rd,rq->dq", flat_one, key_low, preferred_element_type=jnp.float32)
        term_value = jnp.einsum(
            "rd,rq->dq", flat_one, value_low, preferred_element_type=jnp.float32
        )
        grad_normed_one = jnp.einsum(
            "rq,dq->rd", query_low, query_w, preferred_element_type=jnp.float32
        )
        grad_normed_one = grad_normed_one + jnp.einsum(
            "rq,dq->rd", key_low, key_w, preferred_element_type=jnp.float32
        )
        grad_normed_one = grad_normed_one + jnp.einsum(
            "rq,dq->rd", value_low, value_w, preferred_element_type=jnp.float32
        )
        grad_in_part, gain_one_grad = rms_backward(
            grad_normed_one.reshape(seq_count, tok_dev, model_width),
            unit_one,
            inverse_one,
            gain_one.astype(jnp.float32),
        )
        attn_results[layer_index] = (
            lax.psum_scatter(gain_one_grad, ("blk", "head"), scatter_dimension=0, tiled=True),
            lax.psum_scatter(term_query, ("blk", "head"), scatter_dimension=0, tiled=True),
            lax.psum_scatter(term_key, ("blk", "head"), scatter_dimension=0, tiled=True),
            lax.psum_scatter(term_value, ("blk", "head"), scatter_dimension=0, tiled=True),
            lax.psum_scatter(term_out, ("blk", "head"), scatter_dimension=0, tiled=True),
            lax.psum_scatter(gain_two_grad, ("blk", "head"), scatter_dimension=0, tiled=True),
        )
        upstream = grad_middle + grad_in_part

    def stacked(results, member):
        return jnp.stack([entry[member] for entry in results], axis=0)

    return (
        current,
        upstream,
        stacked(attn_results, 0),
        stacked(attn_results, 1),
        stacked(attn_results, 2),
        stacked(attn_results, 3),
        stacked(attn_results, 4),
        stacked(attn_results, 5),
        stacked(ffn_results, 0),
        stacked(ffn_results, 1),
        stacked(ffn_results, 2),
    )


def solution(mesh):
    return jax.shard_map(
        on_device,
        mesh=mesh,
        in_specs=(
            P(None, ("blk", "head"), None),
            P(),
            P(None, ("blk", "head")),
            P(None, ("blk", "head"), None),
            P(None, ("blk", "head"), None),
            P(None, ("blk", "head"), None),
            P(None, ("blk", "head"), None),
            P(None, ("blk", "head")),
            P(None, "blk", "head"),
            P(None, "blk", "head"),
            P(None, "head", "blk"),
            P(None, ("blk", "head"), None),
        ),
        out_specs=(
            P(None, ("blk", "head"), None),
            P(None, ("blk", "head"), None),
            P(None, ("blk", "head")),
            P(None, ("blk", "head"), None),
            P(None, ("blk", "head"), None),
            P(None, ("blk", "head"), None),
            P(None, ("blk", "head"), None),
            P(None, ("blk", "head")),
            P(None, "blk", "head"),
            P(None, "blk", "head"),
            P(None, "head", "blk"),
        ),
        check_vma=False,
    )
```

profile of v0, /device:TPU:0, one launch (start us, length us, event | category | flops | bytes accessed | tf_op | source)
XLA Modules:
  0.0 1849.4 jit_solution(4267469216398412028)
XLA Ops:
  14.2 42.1 %all-reduce.6 = (bf16[2048]{0:T(1024)(128)(2,1)S(1)}, bf16[2048]{0:T(1024)(128)(2,1)S(1)}) all-reduce(bf16[2048]{0:T(1024)(128)(2,1)S(1)} %dynamic-update-slice.24, bf16[2048]{0:T(1024)(128)(2,1)S(1)} %dynamic-update-slice.25), channel_id=2, replica_groups=mesh['blk'=8,'head'=4] {'blk','head'}, use_global_device_ids=true, to_apply=%add.1 | all-reduce | flops 4096 | bytes 16384
  56.8 10.8 all-gather.23.cloned.1.call-done
  69.8 53.5 %all-gather.25.cloned.1.call-done = bf16[1,2048,256]{2,1,0:T(8,128)(2,1)} async-done(((bf16[1,64,256]{2,1,0:T(8,128)(2,1)}), bf16[1,2048,256]{2,1,0:T(8,128)(2,1)}) %all-gather.25.cloned.1.call-update) | async-done | bytes 1048592 | tf_op jit(solution)/shard_map/all_gather | solution.py:87
  129.9 72.5 %all-gather.27.cloned.1.call-done = bf16[1,2048,2048]{2,1,0:T(8,128)(2,1)} async-done(((bf16[1,64,2048]{2,1,0:T(8,128)(2,1)}), bf16[1,2048,2048]{2,1,0:T(8,128)(2,1)}) %all-gather.27.cloned.1.call-update) | async-done | bytes 8388624 | tf_op jit(solution)/shard_map/all_gather | solution.py:85
  202.4 12.3 copy.325
  231.0 17.9 all-to-all-done.1
  262.9 99.9 %while.60 = (s32[]{:T(128)}, bf16[2,256,128]{1,2,0:T(8,128)(2,1)S(1)}, f32[2,8,128]{2,1,0:T(8,128)S(1)}, f32[2,8,128]{2,1,0:T(8,128)S(1)}, f32[2,128,8,64]{1,3,2...) while((s32[]{:T(128)}, ...), condition=%wide.region_33.34_spmd.clone.clone, body=%wide.region_15.33_spmd.clone.clone.sunk | while | flops 276915328 | bytes 19805864 | solution.py:181
  307.3 11.0 collective-permute-start
  376.2 14.9 all-to-all-done.2
  408.4 17.3 all-gather.33.cloned.1.call-done
  425.7 47.8 %all-gather.19.cloned.1.call-done = bf16[2,256,2048]{2,1,0:T(8,128)(2,1)} async-done(((bf16[2,64,2048]{2,1,0:T(8,128)(2,1)}), bf16[2,256,2048]{2,1,0:T(8,128)(2,1)}) %all-gather.19.cloned.1.call-update) | async-done | bytes 2097168 | tf_op jit(solution)/shard_map/all_gather | solution.py:379
  481.7 35.7 %all-gather.31.cloned.1.call-done = bf16[1,2048,1408]{2,1,0:T(8,128)(2,1)} async-done(((bf16[1,256,1408]{2,1,0:T(8,128)(2,1)}), bf16[1,2048,1408]{2,1,0:T(8,128)(2,1)}) %all-gather.31.cloned.1.call-update) | async-done | bytes 5767184 | tf_op jit(solution)/shard_map/all_gather | solution.py:95
  517.5 10.7 multiply_convert_fusion.1
  568.5 11.8 reduce-scatter.12.cloned.1.call-done
  595.9 28.7 %all-to-all-done.3 = bf16[2,64,4,512]{3,1,0,2:T(8,128)(2,1)S(1)} async-done(((bf16[2,64,4,512]{3,1,0,2:T(8,128)(2,1)}), bf16[2,64,4,512]{3,1,0,2:T(8,128)(2,1)S(1)}, u32[]{:S(2)}, u32[]{:S(2)}) %all-to-all-start.3) | async-done | bytes 524320 | tf_op jit(solution)/shard_map/all_to_all | solution.py:494
  627.8 181.0 %while.61 = (s32[]{:T(128)}, f32[2,2,128,8,64]{2,4,3,0,1:T(8,128)S(1)}, f32[2,256,128]{1,2,0:T(8,128)S(1)}, s32[]{:T(128)}, s32[16]{0:T(128)S(1)}, /*index=5*/s3...) while((s32[]{:T(128)}, ...), condition=%wide.region_49.50_spmd.clone.clone, body=%wide.region_39.49_spmd.clone.clone.sunk | while | flops 680068224 | bytes 32126588 | solution.py:296
  735.4 26.7 %collective-permute-done.1 = bf16[2,256,128]{1,2,0:T(8,128)(2,1)S(1)} collective-permute-done((bf16[2,256,128]{1,2,0:T(8,128)(2,1)S(1)}, bf16[2,256,128]{1,2,0:T(8,128)(2,1)S(1)}, u32[]{:S(2)}, u32[]{:S(2)}) %collective-permute-start.1) | collective-permute-done | bytes 131104 | tf_op jit(solution)/shard_map/while/body/eval_jaxpr/ppermute | solution.py:18
  810.3 10.3 all_to_all.87
  834.5 15.6 all_to_all.88
  868.3 52.4 %all-reduce.5 = (f32[2048]{0:T(1024)S(1)}, f32[2048]{0:T(1024)S(1)}) all-reduce(f32[2048]{0:T(1024)S(1)} %get-tuple-element.1738, f32[2048]{0:T(1024)S(1)} %get-tuple-element.1736), channel_id=13, replica_groups=mesh['blk'=8,'head'=4] {'blk','head'}, use_global_device_ids=true, to_apply=%region_53.54.clone | all-reduce | flops 4096 | bytes 32768
  932.2 43.4 %reduce-scatter.16.cloned.1.call-done = f32[64,256]{1,0:T(8,128)} async-done(((f32[2048,256]{1,0:T(8,128)}), f32[64,256]{1,0:T(8,128)}) %reduce-scatter.16.cloned.1.call-update) | async-done | bytes 65552 | tf_op jit(solution)/shard_map/reduce_scatter | solution.py:565
  975.6 140.6 %reduce-scatter.18.cloned.1.call-done = f32[64,256]{1,0:T(8,128)} async-done(((f32[2048,256]{1,0:T(8,128)}), f32[64,256]{1,0:T(8,128)}) %reduce-scatter.18.cloned.1.call-update) | async-done | bytes 65552 | tf_op jit(solution)/shard_map/reduce_scatter | solution.py:566
  1116.3 361.2 %reduce-scatter.20.cloned.1.call-done = f32[64,2048]{1,0:T(8,128)} async-done(((f32[2048,2048]{1,0:T(8,128)}), f32[64,2048]{1,0:T(8,128)}) %reduce-scatter.20.cloned.1.call-update) | async-done | bytes 524304 | tf_op jit(solution)/shard_map/reduce_scatter | solution.py:567
  1477.5 364.7 %reduce-scatter.14.cloned.1.call-done = f32[64,2048]{1,0:T(8,128)} async-done(((f32[2048,2048]{1,0:T(8,128)}), f32[64,2048]{1,0:T(8,128)}) %reduce-scatter.14.cloned.1.call-update) | async-done | bytes 524304 | tf_op jit(solution)/shard_map/reduce_scatter | solution.py:564
  (747 shorter events, 411.8 us)
Async XLA Ops:
  7.2 60.3 %all-gather.23.cloned.1.call-start = ((), (), s32[]{:S(2)}) async-start(), calls=%async_computation.26 | async-start | bytes 1081344 | tf_op jit(solution)/shard_map/all_gather | solution.py:86
  8.0 115.4 %all-gather.25.cloned.1.call-start = ((), (), s32[]{:S(2)}) async-start(), calls=%async_computation.27 | async-start | bytes 1081344 | tf_op jit(solution)/shard_map/all_gather | solution.py:87
  8.7 193.7 %all-gather.27.cloned.1.call-start = ((), (), s32[]{:S(2)}) async-start(), calls=%async_computation.28 | async-start | bytes 8650752 | tf_op jit(solution)/shard_map/all_gather | solution.py:85
  9.4 383.3 %all-gather.29.cloned.1.call-start = ((), (), s32[]{:S(2)}) async-start(), calls=%async_computation.29 | async-start | bytes 8650752 | tf_op jit(solution)/shard_map/all_gather | solution.py:88
  10.0 390.0 %all-gather.21.cloned.1.call-start = ((), (), s32[]{:S(2)}) async-start(), calls=%async_computation.17 | async-start | bytes 2621440 | tf_op jit(solution)/shard_map/all_gather | solution.py:443
  12.2 387.9 %all-gather.35.cloned.1.call-start = ((), (), s32[]{:S(2)}) async-start(), calls=%async_computation.32 | async-start | bytes 6488064 | tf_op jit(solution)/shard_map/all_gather | solution.py:97
  12.8 413.0 %all-gather.33.cloned.1.call-start = ((), (), s32[]{:S(2)}) async-start(), calls=%async_computation.31 | async-start | bytes 6488064 | tf_op jit(solution)/shard_map/all_gather | solution.py:96
  126.3 95.0 %all-to-all-start = ((bf16[2,64,4,128]{3,1,0,2:T(8,128)(2,1)}), bf16[2,64,4,128]{3,1,0,2:T(8,128)(2,1)S(1)}, u32[]{:S(2)}, u32[]{:S(2)}) async-start(bf16[2,64,4,128]{3,1,0,2:T(8,128)(2,1)} %copy.322), calls=%async_computation | async-start | bytes 262144 | tf_op jit(solution)/shard_map/all_to_all | solution.py:363
  221.4 27.6 %all-to-all-start.1 = ((bf16[2,64,4,512]{3,1,0,2:T(8,128)(2,1)}), bf16[2,64,4,512]{3,1,0,2:T(8,128)(2,1)S(1)}, u32[]{:S(2)}, u32[]{:S(2)}) async-start(bf16[2,64,4,512]{3,1,0,2:T(8,128)(2,1)} %copy.326), calls=%async_computation.1 | async-start | bytes 1048576 | tf_op jit(solution)/shard_map/all_to_all | solution.py:356
  307.3 17.5 collective-permute-start
  372.7 18.4 all-to-all-start.2
  376.1 97.4 %all-gather.19.cloned.1.call-start = ((), (), s32[]{:S(2)}) async-start(), calls=%async_computation.15 | async-start | bytes 2621440 | tf_op jit(solution)/shard_map/all_gather | solution.py:379
  398.8 118.6 %all-gather.31.cloned.1.call-start = ((), (), s32[]{:S(2)}) async-start(), calls=%async_computation.30 | async-start | bytes 6488064 | tf_op jit(solution)/shard_map/all_gather | solution.py:95
  399.6 180.8 %reduce-scatter.12.cloned.1.call-start = ((), (), s32[]{:S(2)}) async-start(), calls=%async_computation.18 | async-start | bytes 2621440 | tf_op jit(solution)/shard_map/reduce_scatter | solution.py:466
  536.5 385.3 %reduce-scatter.10.cloned.1.call-start = ((), (), s32[]{:S(2)}) async-start(), calls=%async_computation.16 | async-start | bytes 2621440 | tf_op jit(solution)/shard_map/reduce_scatter | solution.py:390
  544.6 380.7 %reduce-scatter.24.cloned.1.call-start = ((), (), s32[]{:S(2)}) async-start(), calls=%async_computation.24 | async-start | bytes 6488064 | tf_op jit(solution)/shard_map/reduce_scatter | solution.py:476
  552.6 375.0 %reduce-scatter.22.cloned.1.call-start = ((), (), s32[]{:S(2)}) async-start(), calls=%async_computation.23 | async-start | bytes 6488064 | tf_op jit(solution)/shard_map/reduce_scatter | solution.py:473
  560.7 369.2 %reduce-scatter.26.cloned.1.call-start = ((), (), s32[]{:S(2)}) async-start(), calls=%async_computation.25 | async-start | bytes 6488064 | tf_op jit(solution)/shard_map/reduce_scatter | solution.py:479
  591.5 33.1 %all-to-all-start.3 = ((bf16[2,64,4,512]{3,1,0,2:T(8,128)(2,1)}), bf16[2,64,4,512]{3,1,0,2:T(8,128)(2,1)S(1)}, u32[]{:S(2)}, u32[]{:S(2)}) async-start(bf16[2,64,4,512]{3,1,0,2:T(8,128)(2,1)} %copy.350), calls=%async_computation.5 | async-start | bytes 1048576 | tf_op jit(solution)/shard_map/all_to_all | solution.py:494
  595.1 380.5 %reduce-scatter.16.cloned.1.call-start = ((), (), s32[]{:S(2)}) async-start(), calls=%async_computation.20 | async-start | bytes 2162688 | tf_op jit(solution)/shard_map/reduce_scatter | solution.py:565
  728.5 33.6 %collective-permute-start.1 = (bf16[2,256,128]{1,2,0:T(8,128)(2,1)S(1)}, bf16[2,256,128]{1,2,0:T(8,128)(2,1)S(1)}, u32[]{:S(2)}, u32[]{:S(2)}) collective-permute-start(bf16[2,256,128]{1,2,0:T(8,128)(2,1)S(1)} %convert_element_type.542), channel_id=1, source_target_pairs={{0,4},{4,8},{8,12},{12,16},{16,20},{20,24},{24,28},{28,0},{1,5},{5... | collective-permute-start | bytes 393224 | tf_op jit(solution)/shard_map/while/body/eval_jaxpr/ppermute | solution.py:18
  822.9 293.3 %reduce-scatter.18.cloned.1.call-start = ((), (), s32[]{:S(2)}) async-start(), calls=%async_computation.21 | async-start | bytes 2162688 | tf_op jit(solution)/shard_map/reduce_scatter | solution.py:566
  825.1 652.4 %reduce-scatter.20.cloned.1.call-start = ((), (), s32[]{:S(2)}) async-start(), calls=%async_computation.22 | async-start | bytes 17301504 | tf_op jit(solution)/shard_map/reduce_scatter | solution.py:567
  833.7 1008.5 %reduce-scatter.14.cloned.1.call-start = ((), (), s32[]{:S(2)}) async-start(), calls=%async_computation.19 | async-start | bytes 17301504 | tf_op jit(solution)/shard_map/reduce_scatter | solution.py:564
  (45 other events, 752.7 us)
Sparse Core Ops, SparseCore 0:
  11.0 56.5 all-gather.22
  70.5 52.7 all-gather.24
  126.3 76.0 all-gather.26
  205.2 81.0 all-gather.28
  288.2 45.9 all-gather.20
  336.0 44.5 all-gather.34
  382.4 43.2 all-gather.32
  427.8 45.6 all-gather.18
  475.4 41.9 all-gather.30
  536.6 43.6 reduce-scatter.11
  582.6 51.2 reduce-scatter.9
  637.2 60.6 reduce-scatter.23
  701.3 60.8 reduce-scatter.21
  765.5 62.2 reduce-scatter.25
  830.4 145.1 reduce-scatter.15
  978.3 137.9 reduce-scatter.17
  1119.0 358.4 reduce-scatter.19
  1480.2 361.9 reduce-scatter.13
where the time goes:
time: 1860 us; the launch traced here: 1850 us
  waiting for transfers between devices  1300 us (70%)
  matrix products  153 us (8%)
  blocking collectives  120 us (6%)
  loops' own time  100 us (5%)
  local copies, waits for them, and re-layouts  82.1 us (4%)
  starting transfers between devices  42.3 us (2%)
  other arithmetic  35 us (2%)
  between operations  19.6 us (1%)
    reduce_scatter x1, waiting for transfers between devices, on_device(): lax.psum_scatter(term_query, ('blk', 'head'), scatter_dimension=0, tiled=...  365 us
    reduce_scatter x1, waiting for transfers between devices, on_device(): lax.psum_scatter(term_out, ('blk', 'head'), scatter_dimension=0, tiled=True)  361 us
    reduce_scatter x1, waiting for transfers between devices, on_device(): lax.psum_scatter(term_value, ('blk', 'head'), scatter_dimension=0, tiled=...  141 us
    unnamed x2, blocking collectives  94.5 us
    all_gather x1, waiting for transfers between devices, gather_attention(): lax.all_gather(query_w, ('blk', 'head'), axis=0, tiled=True)  72.5 us
    ppermute x15, waiting for transfers between devices, from_behind(): lax.ppermute(shard, axis, [(i, (i + by) % devices) for i in range(devices)])  71.5 us
    all_gather x1, waiting for transfers between devices, gather_attention(): lax.all_gather(value_w, ('blk', 'head'), axis=0, tiled=True)  53.5 us
    all_gather x1, waiting for transfers between devices, on_device(): lax.all_gather(normed_two.astype(jnp.bfloat16), 'head', axis=1, tiled=True)  47.8 us
  transfers between devices with their start and end apart: 37, of which 24 were waited for; matrix products, arithmetic and copies ran while one was open for 13% of the time, Pallas kernels for 0%

commit v1 on v0

v1 whole, which is shorter than its diff:
```python
import functools

import jax
import jax.numpy as jnp
from jax import lax
from jax.experimental import pallas as pl
from jax.experimental.pallas import tpu as pltpu
from jax.sharding import Mesh
from jax.sharding import PartitionSpec as P

HEADS = 32
KV_HEADS = 4
HD = 64
BT = 64
EPS = 1e-05
THETA = 10000.0
NEG = -1e30
LOW = jnp.bfloat16
F32 = jnp.float32

def dot_nt(a, b):
    return lax.dot_general(a, b, (((1,), (1,)), ((), ())), preferred_element_type=jnp.float32)

def dot_nn(a, b):
    return lax.dot_general(a, b, (((1,), (0,)), ((), ())), preferred_element_type=jnp.float32)

def dot_tn(a, b):
    return lax.dot_general(a, b, (((0,), (0,)), ((), ())), preferred_element_type=jnp.float32)

def stack_pairs(block, pairs, scale=None):
    rows = []
    for i in range(pairs):
        part = block[:, 128 * i:128 * i + 128]
        if scale is not None:
            part = part * scale
        lane = lax.broadcasted_iota(jnp.int32, part.shape, 1)
        zero = jnp.zeros_like(part)
        rows.append(jnp.where(lane < HD, part, zero))
        rows.append(jnp.where(lane < HD, zero, part))
    return jnp.concatenate(rows, axis=0)

def sort_keys(order_ref, kv_ref, k2, vv, blocks):
    def body(p, _):
        src = kv_ref[order_ref[p]]
        lane = lax.broadcasted_iota(jnp.int32, src.shape, 1)
        other = pltpu.roll(src.astype(jnp.float32), 64, 1).astype(src.dtype)
        dst = pl.ds(pl.multiple_of(p * BT, BT), BT)
        k2[dst, :] = jnp.where(lane < HD, src, other)
        vv[dst, :] = jnp.where(lane < HD, other, src)
        return 0
    lax.fori_loop(0, blocks, body, 0)

def visible(tile, tk, rows, qp):
    key = tile * tk + lax.broadcasted_iota(jnp.int32, (tk, rows), 0)
    query = qp * BT + (lax.broadcasted_iota(jnp.int32, (tk, rows), 1) & (BT - 1))
    return key <= query

def fwd_kernel(order_ref, qpos_ref, q_ref, kv_ref, o_ref, lse_ref, k2, vv, *, pairs, blocks, tk):
    j = pl.program_id(0)
    rows = pairs * 2 * BT
    @pl.when(j == 0)
    def _():
        sort_keys(order_ref, kv_ref, k2, vv, blocks)
    q8 = stack_pairs(q_ref[...], pairs, jnp.bfloat16(HD ** -0.5))
    qp = qpos_ref[j]
    per = tk // BT
    last = qp // per

    def step(tile, carry, masked):
        m, l, acc = carry
        ds = pl.ds(pl.multiple_of(tile * tk, tk), tk)
        s = dot_nt(k2[ds, :], q8)
        if masked:
            s = jnp.where(visible(tile, tk, rows, qp), s, NEG)
        mn = jnp.maximum(m, jnp.max(s, axis=0, keepdims=True))
        p = jnp.exp(s - mn)
        al = jnp.exp(m - mn)
        l = l * al + jnp.sum(p, axis=0, keepdims=True)
        acc = acc * al + dot_tn(vv[ds, :], p.astype(jnp.bfloat16))
        return mn, l, acc

    init = (jnp.full((1, rows), NEG, jnp.float32), jnp.zeros((1, rows), jnp.float32), jnp.zeros((128, rows), jnp.float32))
    carry = lax.fori_loop(0, last, lambda t, c: step(t, c, False), init)
    m, l, acc = step(last, carry, True)
    lse_ref[...] = (m + jnp.log(l)).reshape(lse_ref.shape)
    out = jnp.transpose(acc / l)
    lane = lax.broadcasted_iota(jnp.int32, (BT, 128), 1)
    for i in range(pairs):
        even = out[2 * i * BT:(2 * i + 1) * BT]
        odd = out[(2 * i + 1) * BT:(2 * i + 2) * BT]
        o_ref[:, 128 * i:128 * i + 128] = jnp.where(lane < HD, even, odd).astype(o_ref.dtype)

def bwd_kernel(order_ref, qpos_ref, q_ref, kv_ref, o_ref, do_ref, lse_ref, dq_ref, dkv_ref, k2, vv, dk, dv, *, pairs, blocks, tk):
    j = pl.program_id(0)
    rows = pairs * 2 * BT
    @pl.when(j == 0)
    def _():
        sort_keys(order_ref, kv_ref, k2, vv, blocks)
        dk[...] = jnp.zeros_like(dk)
        dv[...] = jnp.zeros_like(dv)
    q8 = stack_pairs(q_ref[...], pairs, jnp.bfloat16(HD ** -0.5))
    do8 = stack_pairs(do_ref[...], pairs)
    o8 = stack_pairs(o_ref[...], pairs)
    delta = jnp.sum(do8.astype(jnp.float32) * o8.astype(jnp.float32), axis=1, keepdims=True)
    delta = jnp.transpose(jnp.broadcast_to(delta, (rows, 128)))[:1]
    lse = lse_ref[...].reshape(1, rows)
    qp = qpos_ref[j]
    per = tk // BT
    last = qp // per

    def step(tile, dq, masked):
        ds = pl.ds(pl.multiple_of(tile * tk, tk), tk)
        kt = k2[ds, :]
        s = dot_nt(kt, q8)
        p = jnp.exp(s - lse)
        if masked:
            p = jnp.where(visible(tile, tk, rows, qp), p, 0.0)
        dv[ds, :] += dot_nn(p.astype(jnp.bfloat16), do8)
        dp = dot_nt(vv[ds, :], do8)
        dsc = (p * (dp - delta)).astype(jnp.bfloat16)
        dk[ds, :] += dot_nn(dsc, q8)
        return dq + dot_tn(dsc, kt)

    dq = lax.fori_loop(0, last, lambda t, c: step(t, c, False), jnp.zeros((rows, 128), jnp.float32))
    dq = step(last, dq, True) * (HD ** -0.5)
    lane = lax.broadcasted_iota(jnp.int32, (BT, 128), 1)
    for i in range(pairs):
        even = dq[2 * i * BT:(2 * i + 1) * BT]
        odd = dq[(2 * i + 1) * BT:(2 * i + 2) * BT]
        dq_ref[:, 128 * i:128 * i + 128] = jnp.where(lane < HD, even, odd)

    @pl.when(j == pl.num_programs(0) - 1)
    def _():
        def body(p, _):
            src = pl.ds(pl.multiple_of(p * BT, BT), BT)
            a = dk[src, :]
            b = dv[src, :]
            lane = lax.broadcasted_iota(jnp.int32, a.shape, 1)
            ka = a + pltpu.roll(a, 64, 1)
            vb = b + pltpu.roll(b, 64, 1)
            dkv_ref[order_ref[p]] = jnp.where(lane < HD, ka, vb).astype(dkv_ref.dtype)
            return 0
        lax.fori_loop(0, blocks, body, 0)

def attn_fwd(order, qpos, q, kv, tk=512):
    nq, width = qpos.shape[0], q.shape[1]
    pairs, blocks = width // 128, order.shape[0]
    rows = pairs * 128
    whole = lambda *s: pl.BlockSpec(s, lambda j, *_: (0,) * len(s))
    return pl.pallas_call(
        functools.partial(fwd_kernel, pairs=pairs, blocks=blocks, tk=tk),
        out_shape=(jax.ShapeDtypeStruct(q.shape, jnp.bfloat16), jax.ShapeDtypeStruct((nq, 1, rows), jnp.float32)),
        grid_spec=pltpu.PrefetchScalarGridSpec(
            num_scalar_prefetch=2, grid=(nq,),
            in_specs=[pl.BlockSpec((BT, width), lambda j, *_: (j, 0)), whole(blocks, BT, 128)],
            out_specs=[pl.BlockSpec((BT, width), lambda j, *_: (j, 0)), pl.BlockSpec((1, 1, rows), lambda j, *_: (j, 0, 0))],
            scratch_shapes=[pltpu.VMEM((blocks * BT, 128), jnp.bfloat16)] * 2),
        cost_estimate=pl.CostEstimate(flops=20_000_000_000, bytes_accessed=4 << 20, transcendentals=0),
        name="attn_fwd",
    )(order, qpos, q, kv)

def attn_bwd(order, qpos, q, kv, o, do, lse, tk=512):
    nq, width = qpos.shape[0], q.shape[1]
    pairs, blocks = width // 128, order.shape[0]
    rows = pairs * 128
    whole = lambda *s: pl.BlockSpec(s, lambda j, *_: (0,) * len(s))
    blk = pl.BlockSpec((BT, width), lambda j, *_: (j, 0))
    return pl.pallas_call(
        functools.partial(bwd_kernel, pairs=pairs, blocks=blocks, tk=tk),
        out_shape=(jax.ShapeDtypeStruct(q.shape, jnp.float32), jax.ShapeDtypeStruct((blocks, BT, 128), jnp.bfloat16)),
        grid_spec=pltpu.PrefetchScalarGridSpec(
            num_scalar_prefetch=2, grid=(nq,),
            in_specs=[blk, whole(blocks, BT, 128), blk, blk, pl.BlockSpec((1, 1, rows), lambda j, *_: (j, 0, 0))],
            out_specs=[blk, whole(blocks, BT, 128)],
            scratch_shapes=[pltpu.VMEM((blocks * BT, 128), jnp.bfloat16)] * 2 + [pltpu.VMEM((blocks * BT, 128), jnp.float32)] * 2),
        cost_estimate=pl.CostEstimate(flops=40_000_000_000, bytes_accessed=8 << 20, transcendentals=0),
        name="attn_bwd",
    )(order, qpos, q, kv, o, do, lse)


def turn(x, cos, sin):
    lane = lax.broadcasted_iota(jnp.int32, x.shape, 1) % HD
    partner = jnp.where(lane < HD // 2, pltpu.roll(x, 128 - HD // 2, 1), pltpu.roll(x, HD // 2, 1))
    return x * cos + partner * sin


def rope_kernel(x_ref, cos_ref, sin_ref, q_ref, kv_ref):
    cos, sin = cos_ref[...], sin_ref[...]
    width = q_ref.shape[1]
    for i in range(width // 128):
        part = slice(128 * i, 128 * i + 128)
        q_ref[:, part] = turn(x_ref[:, part], cos, sin).astype(LOW)
    kv = x_ref[:, width:]
    lane = lax.broadcasted_iota(jnp.int32, kv.shape, 1)
    kv_ref[...] = jnp.where(lane < HD, turn(kv, cos, sin), kv).astype(LOW)


def unrope_kernel(dq_ref, dkv_ref, cos_ref, sin_ref, d_ref):
    cos, sin = cos_ref[...], -sin_ref[...]
    width = dq_ref.shape[1]
    for i in range(width // 128):
        part = slice(128 * i, 128 * i + 128)
        d_ref[:, part] = turn(dq_ref[:, part], cos, sin).astype(LOW)
    kv = dkv_ref[...]
    lane = lax.broadcasted_iota(jnp.int32, kv.shape, 1)
    d_ref[:, width:] = jnp.where(lane < HD, turn(kv, cos, sin), kv).astype(LOW)


def rope(x, cos, sin):
    rows, width = x.shape
    tile = lambda w: pl.BlockSpec((128, w), lambda i: (i, 0))
    return pl.pallas_call(
        rope_kernel,
        grid=(rows // 128,),
        in_specs=[tile(width), tile(128), tile(128)],
        out_specs=[tile(width - 128), tile(128)],
        out_shape=(jax.ShapeDtypeStruct((rows, width - 128), LOW), jax.ShapeDtypeStruct((rows, 128), LOW)),
        cost_estimate=pl.CostEstimate(flops=8 * rows * width, bytes_accessed=6 * rows * width, transcendentals=0),
        name="rope",
    )(x, cos, sin)


def unrope(dq, dkv, cos, sin):
    rows, width = dq.shape
    tile = lambda w: pl.BlockSpec((128, w), lambda i: (i, 0))
    return pl.pallas_call(
        unrope_kernel,
        grid=(rows // 128,),
        in_specs=[tile(width), tile(128), tile(128), tile(128)],
        out_specs=tile(width + 128),
        out_shape=jax.ShapeDtypeStruct((rows, width + 128), LOW),
        cost_estimate=pl.CostEstimate(flops=8 * rows * width, bytes_accessed=6 * rows * width, transcendentals=0),
        name="unrope",
    )(dq, dkv, cos, sin)


def swap(value, axis, by=1):
    return lax.ppermute(value, axis, [(i, i ^ by) for i in range(lax.axis_size(axis))])


def onward(value):
    size = lax.axis_size("z")
    return lax.ppermute(value, "z", [(i, (i + 1) % size) for i in range(size)])


def low(value):
    return value.astype(LOW)


def wide(value):
    return value.astype(F32)


def plane_gather(value):
    if lax.axis_size("x") == 2:
        half = value.shape[0] // 2
        from_x, from_y = swap(value, "x"), swap(value, "y")
        top, bottom = swap(from_x[:half], "y"), swap(from_y[half:], "x")
        return [[value], [from_x], [from_y], [top, bottom]]
    row = [value] + [swap(value, "x", d) for d in range(1, lax.axis_size("x"))]
    return [[v] for v in row + [swap(v, "y") for v in row]]


def plane_scatter(parts):
    size = lax.axis_size("x")
    if size == 2:
        half = parts[0].shape[0] // 2
        top, bottom = swap(low(parts[3][:half]), "x"), swap(low(parts[3][half:]), "y")
        to_y = jnp.concatenate([low(wide(parts[2][:half]) + wide(top)), low(parts[2][half:])], 0)
        to_x = jnp.concatenate([low(parts[1][:half]), low(wide(parts[1][half:]) + wide(bottom))], 0)
        return wide(parts[0]) + wide(swap(to_x, "x")) + wide(swap(to_y, "y"))
    kept = [wide(parts[d]) + wide(swap(low(parts[size + d]), "y")) for d in range(size)]
    return sum([wide(swap(low(kept[d]), "x", d)) for d in range(1, size)], kept[0])


def ring_gather(value):
    chunks = [value]
    for _ in range(lax.axis_size("z") - 1):
        chunks.append(onward(chunks[-1]))
    return chunks


def ring_scatter(part_of, kind=LOW):
    size = lax.axis_size("z")
    total = part_of(1)
    for s in list(range(2, size)) + [0]:
        total = wide(part_of(s)) + wide(onward(total.astype(kind)))
    return total


def across(value):
    core = lax.axis_index("c")
    mine = lax.dynamic_index_in_dim(value, core, 0, keepdims=False)
    return jnp.concatenate([mine, swap(lax.dynamic_index_in_dim(value, 1 - core, 0, keepdims=False), "c")], 0)


def back_across(rows):
    core = lax.axis_index("c")
    tokens = rows.shape[0] // 2
    mine, other = rows[:tokens], wide(swap(low(rows[tokens:]), "c"))
    return jnp.stack([jnp.where(core == 0, mine, other), jnp.where(core == 0, other, mine)], 0)


def xor_blocks(value, blk, blocks):
    rows, width = value.shape[:-1], value.shape[-1]
    step = blocks // 2
    bit = 1
    while step >= 1:
        view = value.reshape(rows + (blocks // (2 * step), 2, width * step // blocks))
        flipped = jnp.concatenate([view[..., 1:, :], view[..., :1, :]], -2)
        value = jnp.where((blk // step) % 2 == 1, flipped, view).reshape(rows + (width,))
        step //= 2
    return value


def rms_unit(values):
    inverse = lax.rsqrt(jnp.mean(values * values, axis=-1, keepdims=True) + EPS)
    return values * inverse, inverse


def unit_backward(grad_unit, unit, inverse):
    return inverse * (grad_unit - unit * jnp.mean(grad_unit * unit, axis=-1, keepdims=True))


def place(chunks, rows_of, lead, tail):
    size = lax.axis_size("z")
    core, pos = lax.axis_index("c"), lax.axis_index("z")
    out = jnp.zeros(lead + (2, size) + tail, LOW)
    zeros = (0,) * len(tail)
    for dc in range(2):
        for s in range(size):
            start = (0,) * len(lead) + (core ^ dc, (pos - s) % size) + zeros
            out = lax.dynamic_update_slice(out, chunks[dc][s].reshape(lead + (1, 1) + tail), start)
    return out


def on_device(hidden_in, span_order, attn_gain, w_query, w_key, w_value, w_out, ffn_gain, w_gate, w_up, w_down, cotangent):
    seqs, tok, width = hidden_in.shape
    xs, zs = lax.axis_size("x"), lax.axis_size("z")
    chips = 2 * xs
    yi, xi, core, pos = lax.axis_index("y"), lax.axis_index("x"), lax.axis_index("c"), lax.axis_index("z")
    chip = yi * xs + xi
    blk = chip * 2 + core
    blocks = 2 * chips
    rows = w_query.shape[1]
    heads = HEADS // chips
    q_width = heads * HD
    all_width = q_width + 2 * HD

    per_span = zs // 2
    index = jnp.arange(zs * blocks, dtype=jnp.int32)
    its_blk = (chip ^ (index % blocks // 2)) * 2 + (core ^ (index % 2))
    its_pos = (pos - index // blocks) % zs
    its_span = 2 * its_blk + its_pos // per_span
    spans = jnp.arange(span_order.shape[0], dtype=jnp.int32)
    its_order = jnp.sum(jnp.where(its_span[:, None] == spans[None, :], span_order[None, :], 0), axis=1)
    places = its_order * per_span + its_pos % per_span
    order = jnp.sum(jnp.where(places[None, :] == index[:, None], index[None, :], 0), axis=1)
    query_places = places[:blocks]
    token_pos = (query_places[:, None] * tok + jnp.arange(tok, dtype=jnp.int32)[None, :]).reshape(-1)
    lane = jnp.arange(128, dtype=jnp.int32)
    inverse = 1.0 / THETA ** ((lane % (HD // 2)).astype(F32) * (2.0 / HD))
    angles = token_pos.astype(F32)[:, None] * inverse[None, :]
    cos = jnp.cos(angles)
    sin = jnp.sin(angles) * jnp.where(lane % HD < HD // 2, -1.0, 1.0)[None, :]

    gain_one = wide(attn_gain[0])[:, None]
    kv_of = [g * KV_HEADS // chips for g in range(chips)]
    own_cat = jnp.stack(
        [
            jnp.concatenate(
                [
                    w_query[0, :, g * q_width : (g + 1) * q_width],
                    w_key[0, :, kv_of[g] * HD : (kv_of[g] + 1) * HD],
                    w_value[0, :, kv_of[g] * HD : (kv_of[g] + 1) * HD],
                ],
                1,
            )
            for g in range(chips)
        ],
        0,
    )
    own_cat = low(wide(own_cat) * gain_one[None])

    def exchange(by_chip):
        got = jnp.zeros_like(by_chip)
        for d in range(chips):
            piece = lax.dynamic_index_in_dim(by_chip, chip ^ d, 0, keepdims=True)
            if d % xs:
                piece = swap(piece, "x", d % xs) if d < xs else lax.ppermute(
                    piece, ("y", "x"), [(i, i ^ d) for i in range(chips)]
                )
            elif d:
                piece = swap(piece, "y")
            got = lax.dynamic_update_slice(got, piece, (chip ^ d, 0, 0))
        return got

    by_ring = ring_gather(exchange(own_cat))
    qkv_w = place([by_ring, [swap(v, "c") for v in by_ring]], rows, (chips,), (rows, all_width)).reshape(width, all_width)

    unit_one, inverse_one = rms_unit(hidden_in)
    rows_one = jnp.concatenate(sum(plane_gather(across(low(unit_one))), []), 0)
    projected = jnp.dot(rows_one, qkv_w, preferred_element_type=F32)
    query, kv = rope(projected, cos, sin)
    kv_all = jnp.concatenate([v.reshape(blocks, tok, 2 * HD) for v in ring_gather(kv)], 0)
    attended, log_total = attn_fwd(order, query_places, query, kv_all)

    out_ring = ring_gather(w_out[0])
    out_w = place([out_ring, [swap(v, "c") for v in out_ring]], rows, (), (rows, width)).reshape(q_width, width)
    mixed = jnp.dot(attended, out_w, preferred_element_type=F32)
    chunk = 2 * tok
    middle = hidden_in + back_across(plane_scatter([mixed[d * chunk : (d + 1) * chunk] for d in range(chips)]))

    gain_ring = ring_gather(ffn_gain[0])
    gain_two = jnp.zeros((zs, rows), LOW)
    for s in range(zs):
        gain_two = lax.dynamic_update_slice(gain_two, gain_ring[s][None], ((pos - s) % zs, 0))
    gain_two = wide(gain_two.reshape(zs * rows, 1))

    def ffn_gather(shard):
        pieces = sum(plane_gather(shard), [])
        return jnp.concatenate(pieces + [swap(v, "c") for v in pieces], 0)

    gate_w = ffn_gather(low(wide(w_gate[0]) * gain_two))
    up_w = ffn_gather(low(wide(w_up[0]) * gain_two))
    down_w = ffn_gather(jnp.transpose(w_down[0]))

    rel = core * chips + chip

    def spread(value):
        both = value.reshape(seqs, tok, chips, 2, width // blocks)
        both = jnp.swapaxes(both, 2, 3).reshape(seqs, tok, width)
        both = xor_blocks(both, rel, blocks)
        first, second = ring_gather(both[0]), ring_gather(both[1])
        return jnp.concatenate(sum([[first[s], second[s]] for s in range(zs)], []), 0)

    def gathered_sum(parts):
        sums = jnp.stack([ring_scatter(lambda s, q=q: parts[s, q]) for q in range(seqs)], 0)
        both = xor_blocks(sums, rel, blocks).reshape(seqs, tok, 2, chips, width // blocks)
        return jnp.swapaxes(both, 2, 3).reshape(seqs, tok, width)

    unit_two, inverse_two = rms_unit(middle)
    rows_two = spread(low(unit_two))
    gate = jnp.dot(rows_two, gate_w, preferred_element_type=F32)
    up = jnp.dot(rows_two, up_w, preferred_element_type=F32)
    activated = low(jax.nn.silu(gate) * up)
    partial_out = low(jnp.einsum("rf,df->rd", activated, down_w, preferred_element_type=F32))
    hidden_out = middle + gathered_sum(partial_out.reshape(zs, seqs, tok, width))

    grad_rows = spread(low(cotangent))
    grad_act = jnp.dot(grad_rows, down_w, preferred_element_type=F32)
    sig = jax.nn.sigmoid(gate)
    grad_gate = low(grad_act * up * sig * (1.0 + gate * (1.0 - sig)))
    grad_up = low(grad_act * gate * sig)
    normed_part = low(
        jnp.einsum("rf,df->rd", grad_gate, gate_w, preferred_element_type=F32)
        + jnp.einsum("rf,df->rd", grad_up, up_w, preferred_element_type=F32)
    )
    grad_unit_two = gathered_sum(normed_part.reshape(zs, seqs, tok, width))
    grad_middle = cotangent + unit_backward(grad_unit_two, unit_two, inverse_two)

    def weight_grad(rows_in, rows_f):
        half = width // 2
        sent = low(jnp.einsum("rd,rf->df", rows_in[:, half:], rows_f, preferred_element_type=F32))
        kept = jnp.einsum("rd,rf->df", rows_in[:, :half], rows_f, preferred_element_type=F32)
        both = low(kept + wide(swap(sent, "c")))
        size = half // chips
        return plane_scatter([both[d * size : (d + 1) * size] for d in range(chips)])

    gate_sum = weight_grad(rows_two, grad_gate)
    up_sum = weight_grad(rows_two, grad_up)
    grad_down = jnp.transpose(weight_grad(grad_rows, activated))
    gain_part = jnp.sum(gate_sum * wide(w_gate[0]) + up_sum * wide(w_up[0]), axis=1).reshape(zs, rows)
    grad_ffn_gain = ring_scatter(
        lambda s: lax.dynamic_index_in_dim(gain_part, (pos - s) % zs, 0, keepdims=False), F32
    )

    grad_mid_rows = jnp.concatenate(sum(plane_gather(across(low(grad_middle))), []), 0)
    grad_attended = low(jnp.einsum("rd,qd->rq", grad_mid_rows, out_w, preferred_element_type=F32))
    grad_query, grad_kv = attn_bwd(order, query_places, query, kv_all, attended, grad_attended, log_total)
    grad_kv = ring_scatter(lambda s: grad_kv[s * blocks : (s + 1) * blocks].reshape(blocks * tok, 2 * HD))
    grads = unrope(grad_query, grad_kv, cos, sin)

    def core_ring_sum(full, lead, tail):
        view = full.reshape(lead + (2, zs) + tail)
        axis = len(lead)
        other = lax.dynamic_index_in_dim(view, 1 - core, axis, keepdims=False)
        both = wide(lax.dynamic_index_in_dim(view, core, axis, keepdims=False)) + wide(swap(other, "c"))
        both = low(both)
        return ring_scatter(lambda s: lax.dynamic_index_in_dim(both, (pos - s) % zs, axis, keepdims=False))

    out_part = low(jnp.einsum("rq,rd->qd", attended, grad_mid_rows, preferred_element_type=F32))
    grad_out_w = core_ring_sum(out_part, (), (rows, width))

    unit_part = low(jnp.einsum("rq,dq->rd", grads, qkv_w, preferred_element_type=F32))
    grad_unit_one = back_across(plane_scatter([unit_part[d * chunk : (d + 1) * chunk] for d in range(chips)]))
    grad_in = grad_middle + unit_backward(grad_unit_one, unit_one, inverse_one)

    qkv_part = low(jnp.einsum("rd,rq->dq", rows_one, grads, preferred_element_type=F32))
    qkv_sum = wide(exchange(low(core_ring_sum(qkv_part, (chips,), (rows, all_width)))))
    query_sum = jnp.swapaxes(qkv_sum[:, :, :q_width], 0, 1).reshape(rows, HEADS * HD)
    share = chips // KV_HEADS

    def heads_of(start):
        part = qkv_sum[:, :, start : start + HD].reshape(KV_HEADS, share, rows, HD).sum(1)
        return jnp.swapaxes(part, 0, 1).reshape(rows, KV_HEADS * HD)

    key_sum, value_sum = heads_of(q_width), heads_of(q_width + HD)
    grad_attn_gain = (
        jnp.sum(query_sum * wide(w_query[0]), axis=1)
        + jnp.sum(key_sum * wide(w_key[0]), axis=1)
        + jnp.sum(value_sum * wide(w_value[0]), axis=1)
    )

    return (
        hidden_out,
        grad_in,
        grad_attn_gain[None],
        (query_sum * gain_one)[None],
        (key_sum * gain_one)[None],
        (value_sum * gain_one)[None],
        grad_out_w[None],
        grad_ffn_gain[None],
        (gate_sum * gain_two)[None],
        (up_sum * gain_two)[None],
        grad_down[None],
    )


def solution(mesh):
    n_blk, n_head = mesh.shape["blk"], mesh.shape["head"]
    fine = Mesh(mesh.devices.reshape(2, n_blk // 4, 2, n_head), ("y", "x", "c", "z"))
    blk = ("y", "x", "c")
    every = ("y", "x", "c", "z")
    tokens = P(None, every, None)
    vector = P(None, every)
    return jax.shard_map(
        on_device,
        mesh=fine,
        in_specs=(
            tokens, P(), vector, tokens, tokens, tokens, tokens, vector,
            P(None, blk, "z"), P(None, blk, "z"), P(None, "z", blk), tokens,
        ),
        out_specs=(
            tokens, tokens, vector, tokens, tokens, tokens, tokens, vector,
            P(None, blk, "z"), P(None, blk, "z"), P(None, "z", blk),
        ),
        check_vma=False,
    )
```

time: 1860 us -> 781 us (0.42)
  waiting for transfers between devices: 1300 us -> 337 us
  blocking collectives: 120 us -> 0 us
  loops' own time: 100 us -> 0 us
  local copies, waits for them, and re-layouts: 82.1 us -> 171 us
  matrix products: 153 us -> 64.9 us
  Pallas kernels: 0 us -> 59.6 us
  starting transfers between devices: 42.3 us -> 74.7 us
  other arithmetic: 35 us -> 60.1 us
    reduce_scatter x9 -> x0, waiting for transfers between devices: 922 us -> none  [the longest x1 365 us: on_device(): lax.psum_scatter(term_query, ('blk', 'head'), scatter_dimension=0, tiled=...]
    ppermute x15 -> x126, waiting for transfers between devices: 71.5 us -> 337 us  [the longest x48 197 us: onward(): return lax.ppermute(value, 'z', [(i, (i + 1) % size) for i in range(size)])]
    all_gather x9 -> x0, waiting for transfers between devices: 238 us -> none  [the longest x1 72.5 us: gather_attention(): lax.all_gather(query_w, ('blk', 'head'), axis=0, tiled=True)]
    another operation x64 -> x0, loops' own time: 100 us -> none  [the longest x1 42.4 us: cycle_backward(): return lax.fori_loop(0, cycle_size, cycle_step, (start_query, start_kv))]
    unnamed x2 -> x0, blocking collectives: 94.5 us -> none
    dot_general x140 -> x18, matrix products: 153 us -> 64.9 us  [the longest x3 11.1 us: weight_grad(): jnp.einsum('rd,rf->df', rows_in[:, :half], rows_f, preferred_element_type...]
    all_to_all x4 -> x0, waiting for transfers between devices: 61.5 us -> none  [the longest x1 28.7 us: on_device(): lax.all_to_all(grad_attended.reshape(seq_count, tok_dev, group_size, per_...]
    pallas_call x0 -> x4, Pallas kernels: none -> 59.6 us  [the longest x1 30.4 us: attn_bwd(): pl.pallas_call(functools.partial(bwd_kernel, pairs=pairs, blocks=blocks,...]
  transfers between devices with their start and end apart: 37 -> 126, of which waited for: 24 -> 69; matrix products, arithmetic and copies ran while one was open for 13% -> 27% of each run, Pallas kernels for 0% -> 8%
where the time goes in v1:
time: 781 us; the launch traced here: 771 us
  waiting for transfers between devices  337 us (43%)
  local copies, waits for them, and re-layouts  171 us (22%)
  starting transfers between devices  74.7 us (10%)
  matrix products  64.9 us (8%)
  other arithmetic  60.1 us (8%)
  Pallas kernels  59.6 us (8%)
    ppermute x48, waiting for transfers between devices, onward(): return lax.ppermute(value, 'z', [(i, (i + 1) % size) for i in range(size)])  197 us
    ppermute x76, waiting for transfers between devices, swap(): lax.ppermute(value, axis, [(i, i ^ by) for i in range(lax.axis_size(axis))])  135 us
    unnamed x243, local copies, waits for them, and re-layouts  60.4 us
    ppermute x76, starting transfers between devices, swap(): lax.ppermute(value, axis, [(i, i ^ by) for i in range(lax.axis_size(axis))])  49.6 us
    concatenate x29, local copies, waits for them, and re-layouts, xor_blocks(): flipped = jnp.concatenate([view[..., 1:, :], view[..., :1, :]], -2)  32.7 us
    pallas_call x1, Pallas kernels, attn_bwd(): pl.pallas_call(functools.partial(bwd_kernel, pairs=pairs, blocks=blocks,...  30.4 us
    another operation x26, local copies, waits for them, and re-layouts, gathered_sum(): jnp.stack([ring_scatter(lambda s, q=q: parts[s, q]) for q in range(seqs)]...  22.8 us
    ppermute x48, starting transfers between devices, onward(): return lax.ppermute(value, 'z', [(i, (i + 1) % size) for i in range(size)])  21.5 us
  transfers between devices with their start and end apart: 126, of which 69 were waited for; matrix products, arithmetic and copies ran while one was open for 27% of the time, Pallas kernels for 8%

profile of v1, /device:TPU:0, one launch (start us, length us, event | category | flops | bytes accessed | tf_op | source)
XLA Modules:
  0.0 770.5 jit_solution(4278621088979959480)
XLA Ops:
  72.8 9.0 %collective-permute-done.8 = bf16[4,64,640]{2,1,0:T(8,128)(2,1)S(1)} collective-permute-done((bf16[4,64,640]{2,1,0:T(8,128)(2,1)S(1)}, bf16[4,64,640]{2,1,0:T(8,128)(2,1)S(1)}, u32[]{:S(2)}, u32[]{:S(2)}) %collective-permute-start.8) | collective-permute-done | bytes 327712 | tf_op jit(solution)/shard_map/ppermute | solution.py:243
  107.2 9.6 %collective-permute-done.48 = bf16[256,1408]{1,0:T(8,128)(2,1)} collective-permute-done((bf16[256,1408]{1,0:T(8,128)(2,1)S(1)}, bf16[256,1408]{1,0:T(8,128)(2,1)}, u32[]{:S(2)}, u32[]{:S(2)}) %collective-permute-start.48) | collective-permute-done | bytes 720928 | tf_op jit(solution)/shard_map/ppermute | solution.py:238
  119.7 10.6 %collective-permute-done.39 = bf16[256,1408]{1,0:T(8,128)(2,1)} collective-permute-done((bf16[256,1408]{1,0:T(8,128)(2,1)S(1)}, bf16[256,1408]{1,0:T(8,128)(2,1)}, u32[]{:S(2)}, u32[]{:S(2)}) %collective-permute-start.39) | collective-permute-done | bytes 720928 | tf_op jit(solution)/shard_map/ppermute | solution.py:238
  149.5 10.1 %collective-permute-done.76 = bf16[64,2048]{1,0:T(8,128)(2,1)S(1)} collective-permute-done((bf16[64,2048]{1,0:T(8,128)(2,1)S(1)}, bf16[64,2048]{1,0:T(8,128)(2,1)S(1)}, u32[]{:S(2)}, u32[]{:S(2)}) %collective-permute-start.76) | collective-permute-done | bytes 262176 | tf_op jit(solution)/shard_map/ppermute | solution.py:243
  160.4 8.5 %collective-permute-done.77 = bf16[64,2048]{1,0:T(8,128)(2,1)S(1)} collective-permute-done((bf16[64,2048]{1,0:T(8,128)(2,1)S(1)}, bf16[64,2048]{1,0:T(8,128)(2,1)S(1)}, u32[]{:S(2)}, u32[]{:S(2)}) %collective-permute-start.77) | collective-permute-done | bytes 262176 | tf_op jit(solution)/shard_map/ppermute | solution.py:243
  179.9 9.6 %collective-permute-done.10 = bf16[4,64,640]{2,1,0:T(8,128)(2,1)S(1)} collective-permute-done((bf16[4,64,640]{2,1,0:T(8,128)(2,1)S(1)}, bf16[4,64,640]{2,1,0:T(8,128)(2,1)S(1)}, u32[]{:S(2)}, u32[]{:S(2)}) %collective-permute-start.10) | collective-permute-done | bytes 327712 | tf_op jit(solution)/shard_map/ppermute | solution.py:243
  194.0 7.6 collective-permute-done.59
  216.0 7.0 collective-permute-done.41
  224.5 7.4 collective-permute-done.42
  247.4 6.4 collective-permute-done.15
  253.8 7.7 fusion.91
  270.8 21.3 %attn_fwd.1 = (bf16[512,512]{1,0:T(8,128)(2,1)}, f32[8,1,512]{2,1,0:T(1,128)}) custom-call(s32[32]{0:T(128)} %select_reduce_fusion.order_ref, s32[8]{0:T(128)} %get-tuple-element.197.qpos_ref, bf16[512,512]{1,0:T(8,128)(2,1)} %get-tuple-element.17.q_ref, bf16[32,64,128]{2,1,0:T(8,128)(2,1)} %pad_maximum_fusion.12.kv_ref), custom_call_target="tpu_custom_call" | custom-call | flops 20000000000 | bytes 4194304 | tf_op jit(solution)/shard_map/attn_fwd/pallas_call | solution.py:150
  333.4 9.0 %collective-permute-done.30 = bf16[64,2048]{1,0:T(8,128)(2,1)S(1)} collective-permute-done((bf16[64,2048]{1,0:T(8,128)(2,1)S(1)}, bf16[64,2048]{1,0:T(8,128)(2,1)S(1)}, u32[]{:S(2)}, u32[]{:S(2)}) %collective-permute-start.30) | collective-permute-done | bytes 262176 | tf_op jit(solution)/shard_map/ppermute | solution.py:243
  370.8 6.5 fusion.90
  398.9 9.1 %collective-permute-done.81 = bf16[64,2048]{1,0:T(8,128)(2,1)S(1)} collective-permute-done((bf16[64,2048]{1,0:T(8,128)(2,1)S(1)}, bf16[64,2048]{1,0:T(8,128)(2,1)S(1)}, u32[]{:S(2)}, u32[]{:S(2)}) %collective-permute-start.81) | collective-permute-done | bytes 262176 | tf_op jit(solution)/shard_map/ppermute | solution.py:243
  408.1 11.1 %collective-permute-done.70 = bf16[64,2048]{1,0:T(8,128)(2,1)S(1)} collective-permute-done((bf16[64,2048]{1,0:T(8,128)(2,1)S(1)}, bf16[64,2048]{1,0:T(8,128)(2,1)S(1)}, u32[]{:S(2)}, u32[]{:S(2)}) %collective-permute-start.70) | collective-permute-done | bytes 262176 | tf_op jit(solution)/shard_map/ppermute | solution.py:243
  447.0 7.4 collective-permute-done.79
  548.2 8.3 %collective-permute-done.85 = bf16[128,2048]{1,0:T(8,128)(2,1)S(1)} collective-permute-done((bf16[128,2048]{1,0:T(8,128)(2,1)S(1)}, bf16[128,2048]{1,0:T(8,128)(2,1)S(1)}, u32[]{:S(2)}, u32[]{:S(2)}) %collective-permute-start.85) | collective-permute-done | bytes 524320 | tf_op jit(solution)/shard_map/ppermute | solution.py:238
  568.1 30.4 %attn_bwd.1 = (f32[512,512]{1,0:T(8,128)}, bf16[32,64,128]{2,1,0:T(8,128)(2,1)}) custom-call(s32[32]{0:T(128)} %select_reduce_fusion.order_ref, s32[8]{0:T(128)} %get-tuple-element.197.qpos_ref, bf16[512,512]{1,0:T(8,128)(2,1)} %get-tuple-element.17.q_ref, bf16[32,64,128]{2,1,0:T(8,128)(2,1)} %pad_maximum_fusion.12.kv_ref, ...), custom_call_target="tpu_custom_call" | custom-call | flops 40000000000 | bytes 8388608 | tf_op jit(solution)/shard_map/attn_bwd/pallas_call | solution.py:168
  613.7 6.6 collective-permute-done.91
  681.3 7.5 collective-permute-done.93
  690.1 7.9 %collective-permute-done.105 = bf16[64,2048]{1,0:T(8,128)(2,1)S(1)} collective-permute-done((bf16[64,2048]{1,0:T(8,128)(2,1)S(1)}, bf16[64,2048]{1,0:T(8,128)(2,1)S(1)}, u32[]{:S(2)}, u32[]{:S(2)}) %collective-permute-start.105) | collective-permute-done | bytes 262176 | tf_op jit(solution)/shard_map/ppermute | solution.py:243
  705.9 13.8 %collective-permute-done.115 = bf16[256,1408]{1,0:T(8,128)(2,1)S(1)} collective-permute-done((bf16[256,1408]{1,0:T(8,128)(2,1)S(1)}, bf16[256,1408]{1,0:T(8,128)(2,1)S(1)}, u32[]{:S(2)}, u32[]{:S(2)}) %collective-permute-start.115) | collective-permute-done | bytes 720928 | tf_op jit(solution)/shard_map/ppermute | solution.py:238
  740.5 6.9 collective-permute-done.99
  (772 shorter events, 527.9 us)
Async XLA Ops:
  0.6 65.0 %collective-permute-start.18 = (bf16[64,2048]{1,0:T(8,128)(2,1)}, bf16[64,2048]{1,0:T(8,128)(2,1)}, u32[]{:S(2)}, u32[]{:S(2)}) collective-permute-start(bf16[64,2048]{1,0:T(8,128)(2,1)} %bitcast.416), channel_id=1, source_target_pairs={{0,1},{1,2},{2,3},{3,0},{4,5},{5,6},{6,7},{7,4},{8,9},{9,10},{10,1... | collective-permute-start | bytes 786440 | tf_op jit(solution)/shard_map/ppermute | solution.py:243
  3.7 142.4 %collective-permute-start.21 = (bf16[64,2048]{1,0:T(8,128)(2,1)}, bf16[64,2048]{1,0:T(8,128)(2,1)}, u32[]{:S(2)}, u32[]{:S(2)}) collective-permute-start(bf16[64,2048]{1,0:T(8,128)(2,1)} %bitcast.417), channel_id=1, source_target_pairs={{0,4},{4,0},{1,5},{5,1},{2,6},{6,2},{3,7},{7,3},{8,12},{12,8},{9,1... | collective-permute-start | bytes 786440 | tf_op jit(solution)/shard_map/ppermute | solution.py:238
  3.8 33.9 %collective-permute-start.36 = (bf16[64]{0:T(256)(128)(2,1)}, bf16[64]{0:T(256)(128)(2,1)}, u32[]{:S(2)}, u32[]{:S(2)}) collective-permute-start(bf16[64]{0:T(256)(128)(2,1)} %bitcast.429), channel_id=1, source_target_pairs={{0,1},{1,2},{2,3},{3,0},{4,5},{5,6},{6,7},{7,4},{8,9},{9,10},{10,1... | collective-permute-start | bytes 392 | tf_op jit(solution)/shard_map/ppermute | solution.py:243
  13.9 55.3 %collective-permute-start.72 = (bf16[64,2048]{1,0:T(8,128)(2,1)}, bf16[64,2048]{1,0:T(8,128)(2,1)}, u32[]{:S(2)}, u32[]{:S(2)}) collective-permute-start(bf16[64,2048]{1,0:T(8,128)(2,1)} %squeeze.160), channel_id=1, source_target_pairs={{0,1},{1,2},{2,3},{3,0},{4,5},{5,6},{6,7},{7,4},{8,9},{9,10},{10,1... | collective-permute-start | bytes 786440 | tf_op jit(solution)/shard_map/ppermute | solution.py:243
  16.6 54.5 %collective-permute-start.73 = (bf16[64,2048]{1,0:T(8,128)(2,1)}, bf16[64,2048]{1,0:T(8,128)(2,1)}, u32[]{:S(2)}, u32[]{:S(2)}) collective-permute-start(bf16[64,2048]{1,0:T(8,128)(2,1)} %squeeze.161), channel_id=1, source_target_pairs={{0,1},{1,2},{2,3},{3,0},{4,5},{5,6},{6,7},{7,4},{8,9},{9,10},{10,1... | collective-permute-start | bytes 786440 | tf_op jit(solution)/shard_map/ppermute | solution.py:243
  65.6 33.9 %collective-permute-start.57 = (bf16[256,1408]{0,1:T(8,128)(2,1)S(1)}, bf16[256,1408]{0,1:T(8,128)(2,1)}, u32[]{:S(2)}, u32[]{:S(2)}) collective-permute-start(bf16[256,1408]{0,1:T(8,128)(2,1)S(1)} %bitcast.413), channel_id=1, source_target_pairs={{0,8},{8,0},{1,9},{9,1},{2,10},{10,2},{3,11},{11,3},{4,12},{12,4},... | collective-permute-start | bytes 2162696 | tf_op jit(solution)/shard_map/ppermute | solution.py:238
  93.0 111.8 %collective-permute-start.61 = (bf16[256,1408]{0,1:T(8,128)(2,1)S(1)}, bf16[256,1408]{0,1:T(8,128)(2,1)S(1)}, u32[]{:S(2)}, u32[]{:S(2)}) collective-permute-start(bf16[256,1408]{0,1:T(8,128)(2,1)S(1)} %bitcast.415), channel_id=1, source_target_pairs={{0,4},{4,0},{1,5},{5,1},{2,6},{6,2},{3,7},{7,3},{8,12},{12,8},{9,1... | collective-permute-start | bytes 2162696 | tf_op jit(solution)/shard_map/ppermute | solution.py:238
  118.4 105.8 %collective-permute-start.52 = (bf16[256,1408]{1,0:T(8,128)(2,1)S(1)}, bf16[256,1408]{1,0:T(8,128)(2,1)S(1)}, u32[]{:S(2)}, u32[]{:S(2)}) collective-permute-start(bf16[256,1408]{1,0:T(8,128)(2,1)S(1)} %get-tuple-element.193), channel_id=1, source_target_pairs={{0,4},{4,0},{1,5},{5,1},{2,6},{6,2},{3,7},{7,3},{8,12},{12,8},{9,1... | collective-permute-start | bytes 2162696 | tf_op jit(solution)/shard_map/ppermute | solution.py:238
  160.3 71.6 %collective-permute-start.43 = (bf16[256,1408]{1,0:T(8,128)(2,1)S(1)}, bf16[256,1408]{1,0:T(8,128)(2,1)S(1)}, u32[]{:S(2)}, u32[]{:S(2)}) collective-permute-start(bf16[256,1408]{1,0:T(8,128)(2,1)S(1)} %get-tuple-element.74), channel_id=1, source_target_pairs={{0,4},{4,0},{1,5},{5,1},{2,6},{6,2},{3,7},{7,3},{8,12},{12,8},{9,1... | collective-permute-start | bytes 2162696 | tf_op jit(solution)/shard_map/ppermute | solution.py:238
  201.6 38.8 %collective-permute-start.62 = (bf16[256,1408]{0,1:T(8,128)(2,1)}, bf16[256,1408]{0,1:T(8,128)(2,1)}, u32[]{:S(2)}, u32[]{:S(2)}) collective-permute-start(bf16[256,1408]{0,1:T(8,128)(2,1)} %collective-permute-done.57), channel_id=1, source_target_pairs={{0,4},{4,0},{1,5},{5,1},{2,6},{6,2},{3,7},{7,3},{8,12},{12,8},{9,1... | collective-permute-start | bytes 2162696 | tf_op jit(solution)/shard_map/ppermute | solution.py:238
  224.3 37.2 %collective-permute-start.53 = (bf16[256,1408]{1,0:T(8,128)(2,1)}, bf16[256,1408]{1,0:T(8,128)(2,1)}, u32[]{:S(2)}, u32[]{:S(2)}) collective-permute-start(bf16[256,1408]{1,0:T(8,128)(2,1)} %collective-permute-done.48), channel_id=1, source_target_pairs={{0,4},{4,0},{1,5},{5,1},{2,6},{6,2},{3,7},{7,3},{8,12},{12,8},{9,1... | collective-permute-start | bytes 2162696 | tf_op jit(solution)/shard_map/ppermute | solution.py:238
  231.9 64.6 %collective-permute-start.54 = (bf16[256,1408]{1,0:T(8,128)(2,1)}, bf16[256,1408]{1,0:T(8,128)(2,1)}, u32[]{:S(2)}, u32[]{:S(2)}) collective-permute-start(bf16[256,1408]{1,0:T(8,128)(2,1)} %collective-permute-done.49), channel_id=1, source_target_pairs={{0,4},{4,0},{1,5},{5,1},{2,6},{6,2},{3,7},{7,3},{8,12},{12,8},{9,1... | collective-permute-start | bytes 2162696 | tf_op jit(solution)/shard_map/ppermute | solution.py:238
  233.5 73.6 %collective-permute-start.44 = (bf16[256,1408]{1,0:T(8,128)(2,1)}, bf16[256,1408]{1,0:T(8,128)(2,1)}, u32[]{:S(2)}, u32[]{:S(2)}) collective-permute-start(bf16[256,1408]{1,0:T(8,128)(2,1)} %collective-permute-done.39), channel_id=1, source_target_pairs={{0,4},{4,0},{1,5},{5,1},{2,6},{6,2},{3,7},{7,3},{8,12},{12,8},{9,1... | collective-permute-start | bytes 2162696 | tf_op jit(solution)/shard_map/ppermute | solution.py:238
  245.3 63.8 %collective-permute-start.45 = (bf16[256,1408]{1,0:T(8,128)(2,1)}, bf16[256,1408]{1,0:T(8,128)(2,1)}, u32[]{:S(2)}, u32[]{:S(2)}) collective-permute-start(bf16[256,1408]{1,0:T(8,128)(2,1)} %collective-permute-done.40), channel_id=1, source_target_pairs={{0,4},{4,0},{1,5},{5,1},{2,6},{6,2},{3,7},{7,3},{8,12},{12,8},{9,1... | collective-permute-start | bytes 2162696 | tf_op jit(solution)/shard_map/ppermute | solution.py:238
  261.5 38.2 %collective-permute-start.55 = (bf16[128,1408]{1,0:T(8,128)(2,1)}, bf16[128,1408]{1,0:T(8,128)(2,1)}, u32[]{:S(2)}, u32[]{:S(2)}) collective-permute-start(bf16[128,1408]{1,0:T(8,128)(2,1)} %collective-permute-done.50), channel_id=1, source_target_pairs={{0,4},{4,0},{1,5},{5,1},{2,6},{6,2},{3,7},{7,3},{8,12},{12,8},{9,1... | collective-permute-start | bytes 1081352 | tf_op jit(solution)/shard_map/ppermute | solution.py:238
  385.8 39.8 %collective-permute-start.66 = (bf16[64,2048]{1,0:T(8,128)(2,1)S(1)}, bf16[64,2048]{1,0:T(8,128)(2,1)S(1)}, u32[]{:S(2)}, u32[]{:S(2)}) collective-permute-start(bf16[64,2048]{1,0:T(8,128)(2,1)S(1)} %get-tuple-element.122), channel_id=1, source_target_pairs={{0,1},{1,2},{2,3},{3,0},{4,5},{5,6},{6,7},{7,4},{8,9},{9,10},{10,1... | collective-permute-start | bytes 786440 | tf_op jit(solution)/shard_map/ppermute | solution.py:243
  394.4 39.4 %collective-permute-start.78 = (bf16[64,2048]{1,0:T(8,128)(2,1)}, bf16[64,2048]{1,0:T(8,128)(2,1)S(1)}, u32[]{:S(2)}, u32[]{:S(2)}) collective-permute-start(bf16[64,2048]{1,0:T(8,128)(2,1)} %get-tuple-element.118), channel_id=1, source_target_pairs={{0,1},{1,2},{2,3},{3,0},{4,5},{5,6},{6,7},{7,4},{8,9},{9,10},{10,1... | collective-permute-start | bytes 786440 | tf_op jit(solution)/shard_map/ppermute | solution.py:243
  542.0 92.0 %collective-permute-start.121 = (bf16[1024,1408]{1,0:T(8,128)(2,1)}, bf16[1024,1408]{1,0:T(8,128)(2,1)}, u32[]{:S(2)}, u32[]{:S(2)}) collective-permute-start(bf16[1024,1408]{1,0:T(8,128)(2,1)} %convolution_convert_fusion), channel_id=1, source_target_pairs={{0,4},{4,0},{1,5},{5,1},{2,6},{6,2},{3,7},{7,3},{8,12},{12,8},{9,1... | collective-permute-start | bytes 8650760 | tf_op jit(solution)/shard_map/ppermute | solution.py:238
  603.1 36.3 %collective-permute-start.108 = (bf16[1024,1408]{1,0:T(8,128)(2,1)}, bf16[1024,1408]{1,0:T(8,128)(2,1)}, u32[]{:S(2)}, u32[]{:S(2)}) collective-permute-start(bf16[1024,1408]{1,0:T(8,128)(2,1)} %convolution_convert_fusion.2), channel_id=1, source_target_pairs={{0,4},{4,0},{1,5},{5,1},{2,6},{6,2},{3,7},{7,3},{8,12},{12,8},{9,1... | collective-permute-start | bytes 8650760 | tf_op jit(solution)/shard_map/ppermute | solution.py:238
  603.1 42.6 %collective-permute-start.113 = (bf16[1024,1408]{1,0:T(8,128)(2,1)}, bf16[1024,1408]{1,0:T(8,128)(2,1)}, u32[]{:S(2)}, u32[]{:S(2)}) collective-permute-start(bf16[1024,1408]{1,0:T(8,128)(2,1)} %convolution_convert_fusion.1), channel_id=1, source_target_pairs={{0,4},{4,0},{1,5},{5,1},{2,6},{6,2},{3,7},{7,3},{8,12},{12,8},{9,1... | collective-permute-start | bytes 8650760 | tf_op jit(solution)/shard_map/ppermute | solution.py:238
  613.6 65.1 %collective-permute-start.104 = (bf16[4,64,2048]{2,1,0:T(8,128)(2,1)S(1)}, bf16[4,64,2048]{2,1,0:T(8,128)(2,1)}, u32[]{:S(2)}, u32[]{:S(2)}) collective-permute-start(bf16[4,64,2048]{2,1,0:T(8,128)(2,1)S(1)} %dynamic-slice_bitcast_fusion), channel_id=1, source_target_pairs={{0,4},{4,0},{1,5},{5,1},{2,6},{6,2},{3,7},{7,3},{8,12},{12,8},{9,1... | collective-permute-start | bytes 3145736 | tf_op jit(solution)/shard_map/ppermute | solution.py:238
  631.0 91.3 %collective-permute-start.97 = (bf16[4,4,64,640]{3,2,0,1:T(8,128)(2,1)}, bf16[4,4,64,640]{3,2,0,1:T(8,128)(2,1)}, u32[]{:S(2)}, u32[]{:S(2)}) collective-permute-start(bf16[4,4,64,640]{3,2,0,1:T(8,128)(2,1)} %bitcast.380), channel_id=1, source_target_pairs={{0,4},{4,0},{1,5},{5,1},{2,6},{6,2},{3,7},{7,3},{8,12},{12,8},{9,1... | collective-permute-start | bytes 3932168 | tf_op jit(solution)/shard_map/ppermute | solution.py:238
  704.3 43.3 %collective-permute-start.123 = (bf16[256,1408]{1,0:T(8,128)(2,1)}, bf16[256,1408]{1,0:T(8,128)(2,1)}, u32[]{:S(2)}, u32[]{:S(2)}) collective-permute-start(bf16[256,1408]{1,0:T(8,128)(2,1)} %pad_maximum_fusion.9), channel_id=1, source_target_pairs={{0,8},{8,0},{1,9},{9,1},{2,10},{10,2},{3,11},{11,3},{4,12},{12,4},... | collective-permute-start | bytes 2162696 | tf_op jit(solution)/shard_map/ppermute | solution.py:238
  705.1 42.5 %collective-permute-start.125 = (bf16[256,1408]{1,0:T(8,128)(2,1)}, bf16[256,1408]{1,0:T(8,128)(2,1)}, u32[]{:S(2)}, u32[]{:S(2)}) collective-permute-start(bf16[256,1408]{1,0:T(8,128)(2,1)} %pad_maximum_fusion.10), channel_id=1, source_target_pairs={{0,16},{16,0},{1,17},{17,1},{2,18},{18,2},{3,19},{19,3},{4,20},{20... | collective-permute-start | bytes 2162696 | tf_op jit(solution)/shard_map/ppermute | solution.py:238
  (196 other events, 2055.5 us)
